TPU v7x, 32 devices: a whole 2x2x4 slice. The times are simulated.
32 devices in a mesh: grp: 2 (over x), seq: 16 (over z, y, core).
Axes of the slice: x: 2, y: 2, z: 4, core: 2. Of those that a mesh axis runs over, the one named last changes fastest.
Arguments:
- feats: bfloat16 [32, 128, 384], P('seq', None, 'grp'), may hold values from -6 to 6
- conv_weight: bfloat16 [3, 128, 128], replicated, may hold values from -0.3125 to 0.3125
- conv_bias: float32 [128], replicated, may hold values from -3 to 3
- latent_projection_weight: bfloat16 [16, 128], replicated, may hold values from -0.75 to 0.75
- noise: bfloat16 [32, 16, 384], P('seq', None, 'grp'), may hold values from -6 to 6
- step_index: int32 [1], replicated, may hold values from 0 to 49
- hist: bfloat16 [128, 64], P('seq'), may hold values from -6 to 6
- hist_level: int32 [128], P('seq'), may hold values from 0 to 2
- hist_count: int32 [16], replicated, may hold values from 1 to 8, 96 in all
- w_in: bfloat16 [64, 3072], replicated, may hold values from -2 to 2
- w_hist: bfloat16 [3, 64, 3072], replicated, may hold values from -0.75 to 0.75
- norm_gain: float32 [3072], replicated, may hold values from 0.5 to 2
- w_query: bfloat16 [3072, 1536], P(None, 'grp'), may hold values from -2 to 2
- w_key: bfloat16 [3072, 1536], P(None, 'grp'), may hold values from -2 to 2
- w_value: bfloat16 [3072, 1536], P(None, 'grp'), may hold values from -0.109375 to 0.109375
- q_gain: float32 [128], replicated, may hold values from 0.5 to 6
- k_gain: float32 [128], replicated, may hold values from 0.5 to 6
- w_out: bfloat16 [1536, 3072], P('grp'), may hold values from -0.5 to 0.5
Outputs:
- attention_out: bfloat16 [3072, 3072], P('seq', 'grp')
Inputs may be any that keep to these rules, and one draw needn't show every extreme that they name: hist_count[s] of the 8 history slots of seq index s are live; the largest count is exactly 8.
All inputs are finite; a program needn't handle non-finite values.
Results may differ from a plain program's by a relative error of at most 0.0095.
The roundings to bfloat16 on the way count: a program that leaves them out, or rounds other values in their place, can miss the bound.
Values may be sent and summed in bfloat16 or wider, within the bound.
No kernel may reach another device: no remote copies, remote signals or barrier semaphores. Data moves between devices by JAX's collectives and lax.ppermute only.
A program may use at most 256 MiB of HBM per device.

v0:
```python
import math
import jax
import jax.numpy as jnp
from jax import lax
from jax.sharding import PartitionSpec as P

STEPS = 50
EPSILON = 1e-06


def from_behind(value, axis, steps):
    count = lax.axis_size(axis)
    initial, last = (max(0, -steps), min(count, count - steps))
    return lax.ppermute(value, axis, [(source, source + steps) for source in range(initial, last)])


def time_embed(step_index, width):
    half_width = width // 2
    frequency = jnp.exp(-math.log(10000.0) * jnp.arange(half_width, dtype=jnp.float32) / half_width)
    angles = step_index[0].astype(jnp.float32) * frequency
    return jnp.concatenate([jnp.cos(angles), jnp.sin(angles)])


def rms_scale(values, gain):
    return values * lax.rsqrt(jnp.mean(values * values, axis=-1, keepdims=True) + EPSILON) * gain


def local(
    feats,
    conv_weight,
    conv_bias,
    latent_projection_weight,
    noise,
    step_index,
    hist,
    hist_level,
    hist_count,
    w_in,
    w_hist,
    norm_gain,
    w_query,
    w_key,
    w_value,
    q_gain,
    k_gain,
    w_out,
):
    frame_count, channels, pixels = feats.shape
    earlier = from_behind(feats, "seq", 1)
    padded = jnp.concatenate([earlier, feats], axis=0)
    total = jnp.zeros(feats.shape, jnp.float32)
    for tap_index in range(3):
        window = padded[2 - tap_index : 2 - tap_index + frame_count]
        total = total + jnp.einsum(
            "oc,tcp->top", conv_weight[tap_index], window, preferred_element_type=jnp.float32
        )
    hidden_state = jax.nn.silu(total + conv_bias[None, :, None]).astype(jnp.bfloat16)
    sigma = (STEPS - step_index[0].astype(jnp.float32)) / STEPS
    latent_input = jnp.einsum(
        "qb,zby->zqy", latent_projection_weight, hidden_state, preferred_element_type=jnp.float32
    )
    noisy = ((1.0 - sigma) * latent_input + sigma * noise.astype(jnp.float32)).astype(jnp.bfloat16)
    lat_channels = noisy.shape[1]
    patches = (
        noisy.reshape(frame_count, lat_channels, pixels // 4, 4)
        .transpose(0, 2, 1, 3)
        .reshape(frame_count, pixels // 4, lat_channels * 4)
    )
    width = w_in.shape[1]
    embed = time_embed(step_index, width)
    all_patches = lax.all_gather(patches, "grp", axis=1, tiled=True)
    block_rows = all_patches.shape[1]
    summed = (
        jnp.dot(
            all_patches.reshape(-1, all_patches.shape[2]), w_in, preferred_element_type=jnp.float32
        )
        + embed
    )
    tokens = (
        rms_scale(summed, norm_gain)
        .astype(jnp.bfloat16)
        .reshape(frame_count, block_rows, width)
        .reshape(-1, width)
    )
    history = jnp.zeros((hist.shape[0], width), jnp.float32)
    for level in range(3):
        history = (
            history
            + jnp.dot(hist, w_hist[level], preferred_element_type=jnp.float32)
            * (hist_level == level).astype(jnp.float32)[:, None]
        )
    history = rms_scale(history, norm_gain).astype(jnp.bfloat16)
    both_rows = jnp.concatenate([tokens, history], axis=0)
    sec_rows = tokens.shape[0]
    key_rows = both_rows.shape[0]
    head_size = q_gain.shape[0]
    heads_local = w_query.shape[1] // head_size
    query = rms_scale(
        jnp.dot(tokens, w_query, preferred_element_type=jnp.float32).reshape(
            sec_rows, heads_local, head_size
        ),
        q_gain,
    ).astype(jnp.bfloat16)
    flattened_keys = (
        rms_scale(
            jnp.dot(both_rows, w_key, preferred_element_type=jnp.float32).reshape(
                key_rows, heads_local, head_size
            ),
            k_gain,
        )
        .astype(jnp.bfloat16)
        .reshape(key_rows, heads_local * head_size)
    )
    values_flat = jnp.dot(both_rows, w_value, preferred_element_type=jnp.float32).astype(
        jnp.bfloat16
    )
    seq_count = lax.axis_size("seq")
    shard_ids = jnp.arange(seq_count, dtype=jnp.int32)
    scale = 1.0 / math.sqrt(head_size)
    run_max = jnp.full((heads_local, sec_rows), -1e30, jnp.float32)
    key_piece = lax.all_gather(flattened_keys, "seq", axis=0, tiled=True)
    value_piece = lax.all_gather(values_flat, "seq", axis=0, tiled=True)
    count_rows = key_piece.shape[0]
    row_index = jnp.arange(count_rows, dtype=jnp.int32)
    owner = row_index // key_rows
    local_index = row_index - owner * key_rows
    owner_count = jnp.sum(
        jnp.where(owner[:, None] == shard_ids[None, :], hist_count[None, :], 0), axis=1
    )
    alive = (local_index < sec_rows) | (local_index - sec_rows < owner_count)
    key_heads = key_piece.reshape(count_rows, heads_local, head_size)
    value_heads = value_piece.reshape(count_rows, heads_local, head_size)
    scores = (
        jnp.einsum("qhd,khd->hqk", query, key_heads, preferred_element_type=jnp.float32) * scale
    )
    scores = jnp.where(alive[None, None, :], scores, -1e30)
    new_max = jnp.maximum(run_max, jnp.max(scores, axis=-1))
    soft = jnp.where(alive[None, None, :], jnp.exp(scores - new_max[..., None]), 0.0)
    new_sum = jnp.sum(soft, axis=-1)
    new_weighted = jnp.einsum(
        "hqk,khd->hqd", soft.astype(jnp.bfloat16), value_heads, preferred_element_type=jnp.float32
    )
    attended = new_weighted / new_sum[..., None]
    heads_out = (
        attended.astype(jnp.bfloat16).transpose(1, 0, 2).reshape(sec_rows, heads_local * head_size)
    )
    partial_out = jnp.dot(heads_out, w_out, preferred_element_type=jnp.float32)
    return lax.psum_scatter(
        partial_out.astype(jnp.bfloat16), "grp", scatter_dimension=1, tiled=True
    )


def solution(mesh):
    placed = (
        P("seq", None, "grp"),
        P(),
        P(),
        P(),
        P("seq", None, "grp"),
        P(),
        P("seq", None),
        P("seq"),
        P(),
        P(),
        P(),
        P(),
        P(None, "grp"),
        P(None, "grp"),
        P(None, "grp"),
        P(),
        P(),
        P("grp", None),
    )
    return jax.shard_map(
        local, mesh=mesh, in_specs=placed, out_specs=P("seq", "grp"), check_vma=False
    )
```

profile of v0, /device:TPU:0, one launch (start us, length us, event | category | flops | bytes accessed | tf_op | source)
XLA Modules:
  0.0 191.2 jit_solution(1770931649743177877)
XLA Ops:
  6.5 2.5 %collective-permute-start = (bf16[2,128,192]{1,2,0:T(8,128)(2,1)}, bf16[2,128,192]{1,2,0:T(8,128)(2,1)S(1)}, u32[]{:S(2)}, u32[]{:S(2)}) collective-permute-start(bf16[2,128,192]{1,2,0:T(8,128)(2,1)} %param.18), channel_id=1, source_target_pairs={{0,1},{1,2},{2,3},{3,4},{4,5},{5,6},{6,7},{7,8},{8,9},{9,10},{10,1... | collective-permute-start | bytes 294920 | tf_op jit(solution)/shard_map/ppermute | solution.py:14
  9.8 1.1 fusion.46
  10.9 0.7 compare_convert_fusion
  11.5 1.2 convolution_multiply_fusion.2
  12.7 1.2 fusion.7
  13.9 1.3 multiply_reduce_fusion.2
  15.2 0.7 broadcast_bitcast_fusion
  15.9 0.8 multiply_convert_fusion.3
  16.7 1.0 convolution_add_fusion.2
  17.7 1.1 fusion.15
  19.1 4.8 %all_gather.9 = bf16[2,96,64]{2,0,1:T(2,128)(2,1)S(1)} all-gather(bf16[2,48,64]{2,0,1:T(2,128)(2,1)S(1)} %copy.73), channel_id=1, replica_groups=mesh['grp'=2,'seq'=16] {'grp'}, dimensions={1}, use_global_device_ids=true | all-gather | bytes 36864 | tf_op jit(solution)/shard_map/all_gather | solution.py:71
  24.1 0.6 multiply_reduce_fusion
  24.7 0.3 multiply_convert_fusion
  25.1 1.4 copy-done.5
  26.5 2.0 %fusion.66 = (f32[200,768]{1,0:T(8,128)}, f32[200,768]{1,0:T(8,128)S(1)}) fusion(bf16[3072,768]{1,0:T(8,128)(2,1)S(1)} %copy-done.5, bf16[8,3072]{1,0:T(8,128)(2,1)S(1)} %multiply_convert_fusion.3, bf16[192,3072]{1,0:T(8,128)(2,1)S(1)} %multiply_convert_fusion), kind=kOutput, calls=%fused_computation.94 | convolution fusion | flops 946329600 | bytes 7176192 | tf_op jit(solution)/shard_map/dot_general | solution.py:106
  28.5 1.2 mul.185
  29.7 0.3 reduce_sum.58
  30.2 0.3 mul.186
  30.5 0.9 fusion.27
  31.4 4.2 %convolution_convert_fusion.1 = bf16[200,768]{1,0:T(8,128)(2,1)} fusion(bf16[3072,768]{1,0:T(8,128)(2,1)} %param.32, bf16[8,3072]{1,0:T(8,128)(2,1)S(1)} %multiply_convert_fusion.3, bf16[192,3072]{1,0:T(8,128)(2,1)S(1)} %multiply_convert_fusion), kind=kOutput, calls=%fused_computation.18 | convolution fusion | flops 946329600 | bytes 6254592 | tf_op jit(solution)/shard_map/dot_general | solution.py:114
  35.9 3.4 %fusion.67 = f32[192,768]{1,0:T(8,128)S(1)} fusion(bf16[192,3072]{1,0:T(8,128)(2,1)S(1)} %multiply_convert_fusion, bf16[3072,768]{1,0:T(8,128)(2,1)} %param.30), kind=kOutput, calls=%fused_computation.95 | convolution fusion | flops 905969664 | bytes 6488064 | tf_op jit(solution)/shard_map/dot_general | solution.py:99
  39.4 0.3 multiply_reduce_fusion.1
  39.9 0.3 multiply_convert_fusion.1
  40.2 47.4 %all-gather.3.cloned.1.call-done = bf16[3200,768]{1,0:T(8,128)(2,1)} async-done(((bf16[200,768]{1,0:T(8,128)(2,1)}), bf16[3200,768]{1,0:T(8,128)(2,1)}) %all-gather.3.cloned.1.call-update) | async-done | bytes 4915216 | tf_op jit(solution)/shard_map/all_gather | solution.py:121
  87.6 7.4 %copy.79 = bf16[3200,768]{0,1:T(8,128)(2,1)} copy(bf16[3200,768]{1,0:T(8,128)(2,1)} %all-gather.3.cloned.1.call-done) | data formatting | bytes 9830400 | tf_op jit(solution)/shard_map/all_gather | solution.py:121
  95.1 10.4 %fusion = (f32[6,192]{1,0:T(8,128)S(1)}, f32[6,192,3200]{2,1,0:T(8,128)}) fusion(pred[3200]{0:T(1024)(128)(4,1)S(1)} %fusion.54, bf16[3200,6,128]{0,2,1:T(8,128)(2,1)} %bitcast.85, bf16[192,6,128]{2,1,0:T(8,128)(2,1)S(1)} %multiply_convert_fusion.1), kind=kOutput, calls=%fused_computation.2 | convolution fusion | flops 954776448 | bytes 19963520 | tf_op jit(solution)/shard_map/qhd,khd->hqk/dot_general | solution.py:134
  105.4 9.1 %fusion.1 = f32[6,192]{1,0:T(8,128)S(1)} fusion(f32[6,192,3200]{2,1,0:T(8,128)} %get-tuple-element.15, f32[6,192]{1,0:T(8,128)S(1)} %broadcast_maximum_fusion, pred[3200]{0:T(1024)(128)(4,1)S(1)} %fusion.54), kind=kLoop, calls=%fused_computation.3 | loop fusion | flops 18430848 | bytes 14758016 | tf_op jit(solution)/shard_map/reduce_sum | solution.py:139
  114.5 28.0 %all-gather.5.cloned.1.call-done = bf16[3200,768]{1,0:T(8,128)(2,1)} async-done(((bf16[200,768]{1,0:T(8,128)(2,1)}), bf16[3200,768]{1,0:T(8,128)(2,1)}) %all-gather.5.cloned.1.call-update) | async-done | bytes 4915216 | tf_op jit(solution)/shard_map/all_gather | solution.py:122
  142.5 7.4 %copy.82 = bf16[3200,768]{0,1:T(8,128)(2,1)} copy(bf16[3200,768]{1,0:T(8,128)(2,1)} %all-gather.5.cloned.1.call-done) | data formatting | bytes 9830400 | tf_op jit(solution)/shard_map/all_gather | solution.py:122
  149.9 9.7 %fusion.22 = bf16[6,24,8,128]{3,2,1,0:T(8,128)(2,1)S(1)} fusion(bf16[3200,6,128]{0,2,1:T(8,128)(2,1)} %bitcast.86, f32[6,192,3200]{2,1,0:T(8,128)} %get-tuple-element.15, f32[6,192]{1,0:T(8,128)S(1)} %broadcast_maximum_fusion, pred[3200]{0:T(1024)(128)(4,1)S(1)} %fusion.54, f32[192,6]{0,1:T(8,128)S(1)} %bitcast.90), kind=kOutput, calls=%fused_computation.29 | convolution fusion | flops 962445312 | bytes 19968128 | tf_op jit(solution)/shard_map/hqk,khd->hqd/dot_general | solution.py:140
  159.6 4.4 %convolution_convert_fusion = bf16[192,3072]{1,0:T(8,128)(2,1)} fusion(bf16[768,3072]{1,0:T(8,128)(2,1)} %param.35, bf16[6,24,8,128]{3,2,1,0:T(8,128)(2,1)S(1)} %fusion.22), kind=kOutput, calls=%fused_computation.8 | convolution fusion | flops 906559488 | bytes 6193152 | tf_op jit(solution)/shard_map/dot_general | solution.py:147
  164.1 20.5 %reduce-scatter.2.cloned.1.call-done = bf16[192,1536]{1,0:T(8,128)(2,1)} async-done(((bf16[192,3072]{1,0:T(8,128)(2,1)}), bf16[192,1536]{1,0:T(8,128)(2,1)}) %reduce-scatter.2.cloned.1.call-update) | async-done | bytes 589840 | tf_op jit(solution)/shard_map/reduce_scatter | solution.py:148
  (38 shorter events, 1.5 us)
Async XLA Ops:
  6.5 17.6 %copy-start = (bf16[64,3072]{1,0:T(8,128)(2,1)S(1)}, bf16[64,3072]{1,0:T(8,128)(2,1)}, u32[]{:S(2)}) copy-start(bf16[64,3072]{1,0:T(8,128)(2,1)} %param.27) | copy-start | bytes 1179652
  6.5 18.2 %copy-start.2 = (f32[3072]{0:T(1024)S(1)}, f32[3072]{0:T(1024)}, u32[]{:S(2)}) copy-start(f32[3072]{0:T(1024)} %param.29) | copy-start | bytes 36868
  6.5 81.1 %all-gather.3.cloned.1.call-start = ((), (), s32[]{:S(2)}) async-start(), calls=%async_computation.1 | async-start | bytes 5222400 | tf_op jit(solution)/shard_map/all_gather | solution.py:121
  6.5 10.1 %collective-permute-start = (bf16[2,128,192]{1,2,0:T(8,128)(2,1)}, bf16[2,128,192]{1,2,0:T(8,128)(2,1)S(1)}, u32[]{:S(2)}, u32[]{:S(2)}) collective-permute-start(bf16[2,128,192]{1,2,0:T(8,128)(2,1)} %param.18), channel_id=1, source_target_pairs={{0,1},{1,2},{2,3},{3,4},{4,5},{5,6},{6,7},{7,8},{8,9},{9,10},{10,1... | collective-permute-start | bytes 294920 | tf_op jit(solution)/shard_map/ppermute | solution.py:14
  24.1 2.3 %copy-start.5 = (bf16[3072,768]{1,0:T(8,128)(2,1)S(1)}, bf16[3072,768]{1,0:T(8,128)(2,1)}, u32[]{:S(2)}) copy-start(bf16[3072,768]{1,0:T(8,128)(2,1)} %param.31) | copy-start | bytes 14155780
  30.5 5.3 %copy-start.3 = (s32[16]{0:T(128)S(1)}, s32[16]{0:T(128)}, u32[]{:S(2)}) copy-start(s32[16]{0:T(128)} %param.26) | copy-start | bytes 196
  31.4 111.1 %all-gather.5.cloned.1.call-start = ((), (), s32[]{:S(2)}) async-start(), calls=%async_computation.2 | async-start | bytes 5222400 | tf_op jit(solution)/shard_map/all_gather | solution.py:122
  35.6 4.3 %copy-start.4 = (f32[128]{0:T(128)S(1)}, f32[128]{0:T(128)}, u32[]{:S(2)}) copy-start(f32[128]{0:T(128)} %param.33) | copy-start | bytes 1540
  35.7 149.0 %reduce-scatter.2.cloned.1.call-start = ((), (), s32[]{:S(2)}) async-start(), calls=%async_computation.3 | async-start | bytes 1769472 | tf_op jit(solution)/shard_map/reduce_scatter | solution.py:148
  149.9 34.7 %copy-start.1 = (bf16[64,3072]{1,0:T(8,128)(2,1)S(1)}, bf16[64,3072]{1,0:T(8,128)(2,1)}, u32[]{:S(2)}) copy-start(bf16[64,3072]{1,0:T(8,128)(2,1)} %param.27) | copy-start | bytes 1179652
Sparse Core Ops, SparseCore 0:
  31.5 56.0 all-gather.2
  89.8 52.6 all-gather.4
  164.2 20.3 reduce-scatter.1
where the time goes:
time: 192 us; the launch traced here: 191 us
  waiting for transfers between devices  96 us (50%)
  matrix products  41.5 us (22%)
  local copies, waits for them, and re-layouts  19.5 us (10%)
  between operations  14 us (7%)
  other arithmetic  12.8 us (7%)
  blocking collectives  4.77 us (2%)
  starting transfers between devices  2.61 us (1%)
    all_gather x1, waiting for transfers between devices, local(): key_piece = lax.all_gather(flattened_keys, 'seq', axis=0, tiled=True)  47.4 us
    all_gather x1, waiting for transfers between devices, local(): value_piece = lax.all_gather(values_flat, 'seq', axis=0, tiled=True)  28 us
    reduce_scatter x1, waiting for transfers between devices, local(): lax.psum_scatter(partial_out.astype(jnp.bfloat16), 'grp', scatter_dimensi...  20.5 us
    dot_general x1, matrix products, local(): jnp.einsum('qhd,khd->hqk', query, key_heads, preferred_element_type=jnp.f...  10.4 us
    dot_general x1, matrix products, local(): jnp.einsum('hqk,khd->hqd', soft.astype(jnp.bfloat16), value_heads, prefer...  9.68 us
    reduce_sum x1, other arithmetic, local(): new_sum = jnp.sum(soft, axis=-1)  9.09 us
    all_gather x1, local copies, waits for them, and re-layouts, local(): key_piece = lax.all_gather(flattened_keys, 'seq', axis=0, tiled=True)  7.44 us
    all_gather x1, local copies, waits for them, and re-layouts, local(): value_piece = lax.all_gather(values_flat, 'seq', axis=0, tiled=True)  7.44 us
  transfers between devices with their start and end apart: 4, of which 3 were waited for; matrix products, arithmetic and copies ran while one was open for 22% of the time, Pallas kernels for 0%

commit v1 on v0

--- a/solution.py
+++ b/solution.py
@@ -118,8 +118,13 @@
     shard_ids = jnp.arange(seq_count, dtype=jnp.int32)
     scale = 1.0 / math.sqrt(head_size)
     run_max = jnp.full((heads_local, sec_rows), -1e30, jnp.float32)
-    key_piece = lax.all_gather(flattened_keys, "seq", axis=0, tiled=True)
-    value_piece = lax.all_gather(values_flat, "seq", axis=0, tiled=True)
+    key_piece, value_piece = jnp.split(
+        lax.all_gather(
+            jnp.concatenate([flattened_keys, values_flat], axis=1), "seq", axis=0, tiled=True
+        ),
+        [flattened_keys.shape[1]],
+        axis=1,
+    )
     count_rows = key_piece.shape[0]
     row_index = jnp.arange(count_rows, dtype=jnp.int32)
     owner = row_index // key_rows

time: 192 us -> 203 us (1.057)
  local copies, waits for them, and re-layouts: 19.5 us -> 27.9 us
  waiting for transfers between devices: 96 us -> 101 us
  matrix products: 41.5 us -> 38.3 us
    split x0 -> x3, local copies, waits for them, and re-layouts: none -> 23.1 us  [local(): jnp.split(lax.all_gather(jnp.concatenate([flattened_keys, values_flat], a...]
    all_gather x2 -> x0, local copies, waits for them, and re-layouts: 14.9 us -> none  [the longest x1 7.44 us: local(): key_piece = lax.all_gather(flattened_keys, 'seq', axis=0, tiled=True)]
    all_gather x2 -> x1, waiting for transfers between devices: 75.4 us -> 81 us  [local(): lax.all_gather(jnp.concatenate([flattened_keys, values_flat], axis=1), 's...]
    dot_general x1, matrix products: 4.2 us -> 1.2 us  [local(): jnp.dot(both_rows, w_value, preferred_element_type=jnp.float32)]
  transfers between devices with their start and end apart: 4 -> 3, of which waited for: 3 -> 2; matrix products, arithmetic and copies ran while one was open for 22% -> 6% of each run, Pallas kernels for 0% -> 0%
where the time goes in v1:
time: 203 us; the launch traced here: 202 us
  waiting for transfers between devices  101 us (50%)
  matrix products  38.3 us (19%)
  local copies, waits for them, and re-layouts  27.9 us (14%)
  between operations  14.3 us (7%)
  other arithmetic  12.9 us (6%)
  blocking collectives  4.76 us (2%)
  starting transfers between devices  2.57 us (1%)
    all_gather x1, waiting for transfers between devices, local(): lax.all_gather(jnp.concatenate([flattened_keys, values_flat], axis=1), 's...  81 us
    split x3, local copies, waits for them, and re-layouts, local(): jnp.split(lax.all_gather(jnp.concatenate([flattened_keys, values_flat], a...  23.1 us
    reduce_scatter x1, waiting for transfers between devices, local(): lax.psum_scatter(partial_out.astype(jnp.bfloat16), 'grp', scatter_dimensi...  20.3 us
    dot_general x1, matrix products, local(): jnp.einsum('qhd,khd->hqk', query, key_heads, preferred_element_type=jnp.f...  10.2 us
    dot_general x1, matrix products, local(): jnp.einsum('hqk,khd->hqd', soft.astype(jnp.bfloat16), value_heads, prefer...  9.68 us
    reduce_sum x1, other arithmetic, local(): new_sum = jnp.sum(soft, axis=-1)  9.04 us
    all_gather x1, blocking collectives, local(): all_patches = lax.all_gather(patches, 'grp', axis=1, tiled=True)  4.76 us
    dot_general x1, matrix products, local(): partial_out = jnp.dot(heads_out, w_out, preferred_element_type=jnp.float32)  4.45 us
  transfers between devices with their start and end apart: 3, of which 2 were waited for; matrix products, arithmetic and copies ran while one was open for 6% of the time, Pallas kernels for 0%

profile of v1, /device:TPU:0, one launch (start us, length us, event | category | flops | bytes accessed | tf_op | source)
XLA Modules:
  0.0 202.1 jit_solution(4150988050665385614)
XLA Ops:
  6.5 2.5 %collective-permute-start = (bf16[2,128,192]{1,2,0:T(8,128)(2,1)}, bf16[2,128,192]{1,2,0:T(8,128)(2,1)S(1)}, u32[]{:S(2)}, u32[]{:S(2)}) collective-permute-start(bf16[2,128,192]{1,2,0:T(8,128)(2,1)} %param.18), channel_id=1, source_target_pairs={{0,1},{1,2},{2,3},{3,4},{4,5},{5,6},{6,7},{7,8},{8,9},{9,10},{10,1... | collective-permute-start | bytes 294920 | tf_op jit(solution)/shard_map/ppermute | solution.py:14
  9.8 0.7 compare_convert_fusion
  10.5 0.7 broadcast_bitcast_fusion
  11.1 1.2 convolution_multiply_fusion.2
  12.3 1.2 fusion.7
  13.5 1.3 multiply_reduce_fusion.2
  14.8 1.1 fusion.46
  15.9 0.8 multiply_convert_fusion.3
  16.7 1.0 convolution_add_fusion.2
  17.7 1.1 fusion.15
  19.2 4.8 %all_gather.6 = bf16[2,96,64]{2,0,1:T(2,128)(2,1)S(1)} all-gather(bf16[2,48,64]{2,0,1:T(2,128)(2,1)S(1)} %copy.73), channel_id=1, replica_groups=mesh['grp'=2,'seq'=16] {'grp'}, dimensions={1}, use_global_device_ids=true | all-gather | bytes 36864 | tf_op jit(solution)/shard_map/all_gather | solution.py:71
  24.1 0.6 multiply_reduce_fusion
  24.8 0.3 multiply_convert_fusion
  25.1 1.4 copy-done.5
  26.5 1.2 convolution_convert_fusion.1
  27.9 2.0 %fusion.67 = (f32[200,768]{1,0:T(8,128)}, f32[200,768]{1,0:T(8,128)S(1)}) fusion(bf16[3072,768]{1,0:T(8,128)(2,1)S(1)} %bitcast.92, bf16[8,3072]{1,0:T(8,128)(2,1)S(1)} %multiply_convert_fusion.3, bf16[192,3072]{1,0:T(8,128)(2,1)S(1)} %multiply_convert_fusion), kind=kOutput, calls=%fused_computation.96 | convolution fusion | flops 946329600 | bytes 7176192 | tf_op jit(solution)/shard_map/dot_general | solution.py:106
  30.0 1.2 mul.185
  31.2 0.3 reduce_sum.58
  31.7 0.3 mul.186
  32.1 0.9 pad_maximum_fusion.3
  33.2 3.4 %fusion.68 = f32[192,768]{1,0:T(8,128)S(1)} fusion(bf16[192,3072]{1,0:T(8,128)(2,1)S(1)} %multiply_convert_fusion, bf16[3072,768]{1,0:T(8,128)(2,1)} %param.30), kind=kOutput, calls=%fused_computation.97 | convolution fusion | flops 905969664 | bytes 6488064 | tf_op jit(solution)/shard_map/dot_general | solution.py:99
  36.8 0.3 multiply_reduce_fusion.1
  37.3 0.3 multiply_convert_fusion.1
  37.6 81.0 %all-gather.2.cloned.1.call-done = bf16[3200,1536]{1,0:T(8,128)(2,1)} async-done(((bf16[200,1536]{1,0:T(8,128)(2,1)}), bf16[3200,1536]{1,0:T(8,128)(2,1)}) %all-gather.2.cloned.1.call-update) | async-done | bytes 9830416 | tf_op jit(solution)/shard_map/all_gather | solution.py:122
  118.5 8.3 %fusion.66 = (bf16[3200,768]{1,0:T(8,128)(2,1)}, bf16[3200,768]{1,0:T(8,128)(2,1)}) fusion(bf16[3200,1536]{1,0:T(8,128)(2,1)} %all-gather.2.cloned.1.call-done), kind=kLoop, calls=%fused_computation.95 | loop fusion | bytes 19660800 | tf_op jit(solution)/shard_map/split | solution.py:121
  126.8 7.4 %copy.79 = bf16[3200,768]{0,1:T(8,128)(2,1)} copy(bf16[3200,768]{1,0:T(8,128)(2,1)} %get-tuple-element.5) | data formatting | bytes 9830400 | tf_op jit(solution)/shard_map/split | solution.py:121
  134.2 7.4 %copy.82 = bf16[3200,768]{0,1:T(8,128)(2,1)} copy(bf16[3200,768]{1,0:T(8,128)(2,1)} %get-tuple-element.6) | data formatting | bytes 9830400 | tf_op jit(solution)/shard_map/split | solution.py:121
  141.6 10.2 %fusion = (f32[6,192]{1,0:T(8,128)S(1)}, f32[6,192,3200]{2,1,0:T(8,128)}) fusion(pred[3200]{0:T(1024)(128)(4,1)S(1)} %fusion.54, bf16[3200,6,128]{0,2,1:T(8,128)(2,1)} %bitcast.85, bf16[192,6,128]{2,1,0:T(8,128)(2,1)S(1)} %multiply_convert_fusion.1), kind=kOutput, calls=%fused_computation.2 | convolution fusion | flops 954776448 | bytes 19963520 | tf_op jit(solution)/shard_map/qhd,khd->hqk/dot_general | solution.py:139
  151.8 9.0 %fusion.1 = f32[6,192]{1,0:T(8,128)S(1)} fusion(f32[6,192,3200]{2,1,0:T(8,128)} %get-tuple-element.17, f32[6,192]{1,0:T(8,128)S(1)} %broadcast_maximum_fusion, pred[3200]{0:T(1024)(128)(4,1)S(1)} %fusion.54), kind=kLoop, calls=%fused_computation.3 | loop fusion | flops 18430848 | bytes 14758016 | tf_op jit(solution)/shard_map/reduce_sum | solution.py:144
  160.8 9.7 %fusion.22 = bf16[6,24,8,128]{3,2,1,0:T(8,128)(2,1)S(1)} fusion(bf16[3200,6,128]{0,2,1:T(8,128)(2,1)} %bitcast.86, f32[6,192,3200]{2,1,0:T(8,128)} %get-tuple-element.17, f32[6,192]{1,0:T(8,128)S(1)} %broadcast_maximum_fusion, pred[3200]{0:T(1024)(128)(4,1)S(1)} %fusion.54, f32[192,6]{0,1:T(8,128)S(1)} %bitcast.90), kind=kOutput, calls=%fused_computation.29 | convolution fusion | flops 962445312 | bytes 19968128 | tf_op jit(solution)/shard_map/hqk,khd->hqd/dot_general | solution.py:145
  170.5 4.4 %convolution_convert_fusion = bf16[192,3072]{1,0:T(8,128)(2,1)} fusion(bf16[768,3072]{1,0:T(8,128)(2,1)} %param.35, bf16[6,24,8,128]{3,2,1,0:T(8,128)(2,1)S(1)} %fusion.22), kind=kOutput, calls=%fused_computation.8 | convolution fusion | flops 906559488 | bytes 6193152 | tf_op jit(solution)/shard_map/dot_general | solution.py:152
  175.0 20.3 %reduce-scatter.2.cloned.1.call-done = bf16[192,1536]{1,0:T(8,128)(2,1)} async-done(((bf16[192,3072]{1,0:T(8,128)(2,1)}), bf16[192,1536]{1,0:T(8,128)(2,1)}) %reduce-scatter.2.cloned.1.call-update) | async-done | bytes 589840 | tf_op jit(solution)/shard_map/reduce_scatter | solution.py:153
  (42 shorter events, 1.9 us)
Async XLA Ops:
  6.5 17.6 %copy-start = (bf16[64,3072]{1,0:T(8,128)(2,1)S(1)}, bf16[64,3072]{1,0:T(8,128)(2,1)}, u32[]{:S(2)}) copy-start(bf16[64,3072]{1,0:T(8,128)(2,1)} %param.27) | copy-start | bytes 1179652
  6.5 18.2 %copy-start.2 = (f32[3072]{0:T(1024)S(1)}, f32[3072]{0:T(1024)}, u32[]{:S(2)}) copy-start(f32[3072]{0:T(1024)} %param.29) | copy-start | bytes 36868
  6.5 112.0 %all-gather.2.cloned.1.call-start = ((), (), s32[]{:S(2)}) async-start(), calls=%async_computation.1 | async-start | bytes 10444800 | tf_op jit(solution)/shard_map/all_gather | solution.py:122
  6.5 10.1 %collective-permute-start = (bf16[2,128,192]{1,2,0:T(8,128)(2,1)}, bf16[2,128,192]{1,2,0:T(8,128)(2,1)S(1)}, u32[]{:S(2)}, u32[]{:S(2)}) collective-permute-start(bf16[2,128,192]{1,2,0:T(8,128)(2,1)} %param.18), channel_id=1, source_target_pairs={{0,1},{1,2},{2,3},{3,4},{4,5},{5,6},{6,7},{7,8},{8,9},{9,10},{10,1... | collective-permute-start | bytes 294920 | tf_op jit(solution)/shard_map/ppermute | solution.py:14
  24.1 2.3 %copy-start.5 = (bf16[3072,768]{1,0:T(8,128)(2,1)S(1)}, bf16[3072,768]{1,0:T(8,128)(2,1)}, u32[]{:S(2)}) copy-start(bf16[3072,768]{1,0:T(8,128)(2,1)} %param.32) | copy-start | bytes 14155780
  24.7 3.2 %slice-start = ((s8[4718592]{0:T(1024)(128)(4,1)}), s8[4194304]{0:T(1024)(128)(4,1)S(1)}, s32[]{:S(2)}) async-start(s8[4718592]{0:T(1024)(128)(4,1)} %bitcast.91), calls=%async_computation.3 | async-start | bytes 8388608
  26.5 1.5 slice-start.1
  30.0 3.1 %copy-start.3 = (s32[16]{0:T(128)S(1)}, s32[16]{0:T(128)}, u32[]{:S(2)}) copy-start(s32[16]{0:T(128)} %param.26) | copy-start | bytes 196
  33.0 4.3 %copy-start.4 = (f32[128]{0:T(128)S(1)}, f32[128]{0:T(128)}, u32[]{:S(2)}) copy-start(f32[128]{0:T(128)} %param.33) | copy-start | bytes 1540
  33.0 162.3 %reduce-scatter.2.cloned.1.call-start = ((), (), s32[]{:S(2)}) async-start(), calls=%async_computation.2 | async-start | bytes 1769472 | tf_op jit(solution)/shard_map/reduce_scatter | solution.py:153
  160.8 34.5 %copy-start.1 = (bf16[64,3072]{1,0:T(8,128)(2,1)S(1)}, bf16[64,3072]{1,0:T(8,128)(2,1)}, u32[]{:S(2)}) copy-start(bf16[64,3072]{1,0:T(8,128)(2,1)} %param.27) | copy-start | bytes 1179652
Sparse Core Ops, SparseCore 0:
  33.1 85.3 all-gather.1
  175.1 20.1 reduce-scatter.1
